TPU v7x, 128 devices: a whole 4x4x4 slice. The times are simulated.
128 devices in a mesh: section: 2 (over z_lo), dp: 16 (over y, x), tensor: 4 (over z_hi, core).
Axes of the slice: x: 4, y: 4, z: 4 (z_hi: 2, z_lo: 2; z = z_hi * 2 + z_lo), core: 2. Of those that a mesh axis runs over, the one named last changes fastest.
Arguments:
- images: bfloat16 [48, 577, 768], P('dp', None, 'tensor'), may hold values from -6 to 6
- slot_table: int32 [32], P('dp'), may hold values from 0 to 3, as said below
- ln1_gain: float32 [2, 768], P('section'), may hold values from 0.5 to 1.5
- ln1_bias: float32 [2, 768], P('section'), may hold values from -1.5 to 1.5
- qkv_weight: bfloat16 [2, 768, 3, 768], P('section', None, None, 'tensor'), may hold values from -0.21875 to 0.21875
- qv_bias: float32 [2, 2, 768], P('section', None, 'tensor'), may hold values from -1.5 to 1.5
- out_weight: bfloat16 [2, 768, 768], P('section', 'tensor'), may hold values from -0.875 to 0.875
- out_bias: float32 [2, 768], P('section'), may hold values from -1.5 to 1.5
- ln2_gain: float32 [2, 768], P('section'), may hold values from 0.5 to 1.5
- ln2_bias: float32 [2, 768], P('section'), may hold values from -1.5 to 1.5
- fc1_weight: bfloat16 [2, 768, 3072], P('section', None, 'tensor'), may hold values from -0.21875 to 0.21875
- fc1_bias: float32 [2, 3072], P('section', 'tensor'), may hold values from -1.5 to 1.5
- fc2_weight: bfloat16 [2, 3072, 768], P('section', 'tensor'), may hold values from -0.109375 to 0.109375
- fc2_bias: float32 [2, 768], P('section'), may hold values from -1.5 to 1.5
- cotangent: bfloat16 [48, 577, 768], P('dp', None, 'tensor'), may hold values from -6 to 6
Outputs:
- activations: bfloat16 [2, 48, 577, 768], P('section', 'dp', None, 'tensor')
- input_grads: float32 [2, 48, 577, 768], P('section', 'dp', None, 'tensor')
- ln1_gain_grad: float32 [2, 768], P('section', 'tensor')
- ln1_bias_grad: float32 [2, 768], P('section', 'tensor')
- qkv_weight_grad: float32 [2, 768, 3, 768], P('section', None, None, 'tensor')
- qv_bias_grad: float32 [2, 2, 768], P('section', None, 'tensor')
- out_weight_grad: float32 [2, 768, 768], P('section', 'tensor')
- out_bias_grad: float32 [2, 768], P('section', 'tensor')
- ln2_gain_grad: float32 [2, 768], P('section', 'tensor')
- ln2_bias_grad: float32 [2, 768], P('section', 'tensor')
- fc1_weight_grad: float32 [2, 768, 3072], P('section', None, 'tensor')
- fc1_bias_grad: float32 [2, 3072], P('section', 'tensor')
- fc2_weight_grad: float32 [2, 3072, 768], P('section', 'tensor')
- fc2_bias_grad: float32 [2, 768], P('section', 'tensor')
Inputs may be any that keep to these rules, and one draw needn't show every extreme that they name: `slot_table`: within one data member's 2 entries, values below 3 are distinct; the value 3 means that the micro-batch has no image there.
All inputs are finite; a program needn't handle non-finite values.
Results may differ from a plain program's by a relative error of at most 0.0095.
Values may be sent and summed in bfloat16 or wider, within the bound.
No kernel may reach another device: no remote copies, remote signals or barrier semaphores. Data moves between devices by JAX's collectives and lax.ppermute only.
A program may use at most 192 MiB of HBM per device.

v0:
```python
from functools import partial
import jax
import jax.numpy as jnp
from jax import lax
from jax.sharding import PartitionSpec as P

HD = 64
epsilon = 1e-06


def shifted(block, axis, distance):
    devices = range(lax.axis_size(axis))
    route = [(i - distance, i) for i in devices if i - distance in devices]
    return lax.ppermute(block, axis, route)


def standardize_rows(values):
    row_means = jnp.mean(values, axis=1, keepdims=True)
    center = values - row_means
    inverse = lax.rsqrt(jnp.mean(center * center, axis=1, keepdims=True) + epsilon)
    return (center * inverse, row_means, inverse)


def contract_rows(left_side, right_side):
    return lax.dot_general(
        left_side, right_side, (((0,), (0,)), ((), ())), preferred_element_type=jnp.float32
    )


def contract_cols(left_side, right_side):
    return lax.dot_general(
        left_side, right_side, (((1,), (1,)), ((), ())), preferred_element_type=jnp.float32
    )


def member_sum(gradients):
    return lax.psum(gradients, "dp")


def tensor_scatter_sum(partial_value):
    group = lax.axis_size("tensor")
    rows_count, full_width = partial_value.shape
    pieces = lax.all_to_all(partial_value.astype(jnp.bfloat16), "tensor", 1, 0, tiled=True).reshape(
        group, rows_count, full_width // group
    )
    return jnp.sum(pieces.astype(jnp.float32), axis=0)


def tensor_sum(partial_value):
    summed = tensor_scatter_sum(partial_value)
    return lax.all_gather(summed.astype(jnp.bfloat16), "tensor", axis=1, tiled=True).astype(
        jnp.float32
    )


def layer_forward(partial_residual, params, column):
    (
        first_norm_gain,
        first_norm_bias,
        qkv_mat,
        qv_add,
        out_mat,
        out_add,
        second_norm_gain,
        second_norm_bias,
        up_mat,
        up_add,
        down_mat,
        down_add,
    ) = params
    rows_count = partial_residual.shape[0]
    part_width = partial_residual.shape[1]
    hidden_width = first_norm_gain.shape[0]
    head_count = part_width // HD
    complete_residual = lax.all_gather(partial_residual, "tensor", axis=1, tiled=True).astype(
        jnp.float32
    )
    first_centered_unit, first_row_averages, first_inverse_deviation = standardize_rows(
        complete_residual
    )
    first_normalized = (first_centered_unit * first_norm_gain + first_norm_bias).astype(
        jnp.bfloat16
    )
    projected = jnp.dot(
        first_normalized,
        qkv_mat.reshape(hidden_width, 3 * part_width),
        preferred_element_type=jnp.float32,
    ).reshape(rows_count, 3, part_width)
    queries = (projected[:, 0] + qv_add[0]).astype(jnp.bfloat16).reshape(rows_count, head_count, HD)
    keys_part = projected[:, 1].astype(jnp.bfloat16).reshape(rows_count, head_count, HD)
    values_part = (
        (projected[:, 2] + qv_add[1]).astype(jnp.bfloat16).reshape(rows_count, head_count, HD)
    )
    scores = jnp.einsum(
        "qhd,khd->hqk", queries, keys_part, preferred_element_type=jnp.float32
    ) * HD ** (-0.5)
    totals = jax.nn.logsumexp(scores, axis=2, keepdims=True)
    probabilities = jnp.exp(scores - totals)
    attended = (
        jnp.einsum(
            "hqk,khd->qhd",
            probabilities.astype(jnp.bfloat16),
            values_part,
            preferred_element_type=jnp.float32,
        )
        .reshape(rows_count, part_width)
        .astype(jnp.bfloat16)
    )
    branch = tensor_sum(jnp.dot(attended, out_mat, preferred_element_type=jnp.float32))
    middle = complete_residual + branch + out_add
    middle_rounded = middle.astype(jnp.bfloat16).astype(jnp.float32)
    second_centered_unit, second_row_averages, second_inverse_deviation = standardize_rows(
        middle_rounded
    )
    second_normalized = (second_centered_unit * second_norm_gain + second_norm_bias).astype(
        jnp.bfloat16
    )
    hidden_pre = jnp.dot(second_normalized, up_mat, preferred_element_type=jnp.float32) + up_add
    hidden = jax.nn.gelu(hidden_pre, approximate=False).astype(jnp.bfloat16)
    feed_out = tensor_scatter_sum(jnp.dot(hidden, down_mat, preferred_element_type=jnp.float32))
    result_part = (
        lax.dynamic_slice_in_dim(middle, column, part_width, 1)
        + feed_out
        + lax.dynamic_slice_in_dim(down_add, column, part_width, 0)
    )
    saved_state = (
        first_centered_unit,
        first_inverse_deviation,
        first_normalized,
        queries,
        keys_part,
        values_part,
        totals,
        attended,
        second_centered_unit,
        second_inverse_deviation,
        second_normalized,
        hidden_pre,
        hidden,
    )
    return (result_part.astype(jnp.bfloat16), saved_state)


def layer_backward(grad_part, saved_state, params, column, grad_sums):
    (
        first_norm_gain,
        first_norm_bias,
        qkv_mat,
        qv_add,
        out_mat,
        out_add,
        second_norm_gain,
        second_norm_bias,
        up_mat,
        up_add,
        down_mat,
        down_add,
    ) = params
    (
        first_centered_unit,
        first_inverse_deviation,
        first_normalized,
        queries,
        keys_part,
        values_part,
        totals,
        attended,
        second_centered_unit,
        second_inverse_deviation,
        second_normalized,
        hidden_pre,
        hidden,
    ) = saved_state
    rows_count = grad_part.shape[0]
    part_width = grad_part.shape[1]
    hidden_width = first_norm_gain.shape[0]
    head_count = part_width // HD

    def local_cols(matrix):
        return lax.dynamic_slice_in_dim(matrix, column, part_width, 1)

    grad_full_bf16 = lax.all_gather(grad_part, "tensor", axis=1, tiled=True)
    grad_full = grad_full_bf16.astype(jnp.float32)
    down_grad = contract_rows(hidden, grad_full_bf16)
    down_add_grad = jnp.sum(local_cols(grad_full), axis=0)
    hidden_grad = contract_cols(grad_full_bf16, down_mat)
    unused_value, gelu_back = jax.vjp(partial(jax.nn.gelu, approximate=False), hidden_pre)
    pre_grad = gelu_back(hidden_grad)[0].astype(jnp.bfloat16)
    up_grad = contract_rows(second_normalized, pre_grad)
    up_add_grad = jnp.sum(pre_grad.astype(jnp.float32), axis=0)
    normalized_gradient = tensor_sum(contract_cols(pre_grad, up_mat))
    second_gain_gradient = jnp.sum(local_cols(normalized_gradient * second_centered_unit), axis=0)
    bias_two_grad = jnp.sum(local_cols(normalized_gradient), axis=0)
    second_rescaled = normalized_gradient * second_norm_gain
    first_running_total = jnp.sum(second_rescaled, axis=1, keepdims=True)
    second_running_total = jnp.sum(second_rescaled * second_centered_unit, axis=1, keepdims=True)
    middle_grad = grad_full + second_inverse_deviation * (
        second_rescaled
        - first_running_total / hidden_width
        - second_centered_unit * second_running_total / hidden_width
    )
    feed_grads = (
        second_gain_gradient,
        bias_two_grad,
        up_grad,
        up_add_grad,
        down_grad,
        down_add_grad,
    )
    feed_grads = tuple((older + newer for older, newer in zip(grad_sums[6:], feed_grads)))
    branch_grad = middle_grad.astype(jnp.bfloat16)
    out_grad = contract_rows(attended, branch_grad)
    out_add_grad = jnp.sum(local_cols(middle_grad), axis=0)
    attended_grad = (
        contract_cols(branch_grad, out_mat).astype(jnp.bfloat16).reshape(rows_count, head_count, HD)
    )
    scale_factor = HD ** (-0.5)
    scores = (
        jnp.einsum("qhd,khd->hqk", queries, keys_part, preferred_element_type=jnp.float32)
        * scale_factor
    )
    probabilities = jnp.exp(scores - totals)
    values_grad = jnp.einsum(
        "hqk,qhd->khd",
        probabilities.astype(jnp.bfloat16),
        attended_grad,
        preferred_element_type=jnp.float32,
    )
    weight_grad = jnp.einsum(
        "qhd,khd->hqk", attended_grad, values_part, preferred_element_type=jnp.float32
    )
    rowdot = jnp.sum(probabilities * weight_grad, axis=2, keepdims=True)
    score_grad = (probabilities * (weight_grad - rowdot)).astype(jnp.bfloat16)
    query_grad = (
        jnp.einsum("hqk,khd->qhd", score_grad, keys_part, preferred_element_type=jnp.float32)
        * scale_factor
    )
    key_grad = (
        jnp.einsum("hqk,qhd->khd", score_grad, queries, preferred_element_type=jnp.float32)
        * scale_factor
    )
    projected_grad = jnp.stack(
        [
            query_grad.reshape(rows_count, part_width),
            key_grad.reshape(rows_count, part_width),
            values_grad.reshape(rows_count, part_width),
        ],
        axis=1,
    ).astype(jnp.bfloat16)
    flat_grad = projected_grad.reshape(rows_count, 3 * part_width)
    qkv_grad = contract_rows(first_normalized, flat_grad).reshape(hidden_width, 3, part_width)
    qv_add_grad = jnp.stack(
        [
            jnp.sum(projected_grad[:, 0].astype(jnp.float32), axis=0),
            jnp.sum(projected_grad[:, 2].astype(jnp.float32), axis=0),
        ]
    )
    first_normalized_gradient = tensor_sum(
        contract_cols(flat_grad, qkv_mat.reshape(hidden_width, 3 * part_width))
    )
    first_gain_gradient = jnp.sum(
        local_cols(first_normalized_gradient * first_centered_unit), axis=0
    )
    bias_one_grad = jnp.sum(local_cols(first_normalized_gradient), axis=0)
    first_rescaled = first_normalized_gradient * first_norm_gain
    third_running_total = jnp.sum(first_rescaled, axis=1, keepdims=True)
    fourth_running_total = jnp.sum(first_rescaled * first_centered_unit, axis=1, keepdims=True)
    stream_grad = middle_grad + first_inverse_deviation * (
        first_rescaled
        - third_running_total / hidden_width
        - first_centered_unit * fourth_running_total / hidden_width
    )
    attention_grads = (
        first_gain_gradient,
        bias_one_grad,
        qkv_grad,
        qv_add_grad,
        out_grad,
        out_add_grad,
    )
    attention_grads = tuple((older + newer for older, newer in zip(grad_sums[:6], attention_grads)))
    return (local_cols(stream_grad), attention_grads + feed_grads)


def shards(
    images,
    slot_table,
    ln1_gain,
    ln1_bias,
    qkv_weight,
    qv_bias,
    out_weight,
    out_bias,
    ln2_gain,
    ln2_bias,
    fc1_weight,
    fc1_bias,
    fc2_weight,
    fc2_bias,
    cotangent,
):
    params = tuple(
        (
            weight_arg[0]
            for weight_arg in (
                ln1_gain,
                ln1_bias,
                qkv_weight,
                qv_bias,
                out_weight,
                out_bias,
                ln2_gain,
                ln2_bias,
                fc1_weight,
                fc1_bias,
                fc2_weight,
                fc2_bias,
            )
        )
    )
    section_index = lax.axis_index("section")
    part_width = images.shape[2]
    column = lax.axis_index("tensor") * part_width
    slot_count = images.shape[0]
    micro_count = slot_table.shape[0]
    slot_ids = jnp.arange(slot_count, dtype=jnp.int32)

    def locate(batch_index):
        clipped = jnp.clip(batch_index, 0, micro_count - 1)
        chosen = lax.dynamic_index_in_dim(slot_table, clipped, 0, keepdims=False)
        active = (batch_index >= 0) & (batch_index < micro_count) & (chosen < slot_count)
        return (jnp.minimum(chosen, slot_count - 1), active, (slot_ids == chosen) & active)

    received = jnp.zeros(images.shape[1:], jnp.bfloat16)
    layer_outputs = jnp.zeros(images.shape, jnp.bfloat16)
    saved_states = []
    for step_index in range(micro_count + 1):
        where_from, active, placed = locate(step_index - section_index)
        own_image = lax.dynamic_index_in_dim(images, where_from, 0, keepdims=False)
        entering = jnp.where(section_index == 0, own_image, received)
        leaving, layer_state = layer_forward(entering, params, column)
        saved_states.append(layer_state)
        layer_outputs = layer_outputs + placed[:, None, None].astype(jnp.bfloat16) * leaving[None]
        if step_index < micro_count:
            received = shifted(leaving, "section", 1)

    def zeros_of(extent):
        return jnp.zeros(extent, jnp.float32)

    grad_sums = (
        zeros_of((part_width,)),
        zeros_of((part_width,)),
        zeros_of(params[2].shape),
        zeros_of(params[3].shape),
        zeros_of(params[4].shape),
        zeros_of((part_width,)),
        zeros_of((part_width,)),
        zeros_of((part_width,)),
        zeros_of(params[8].shape),
        zeros_of(params[9].shape),
        zeros_of(params[10].shape),
        zeros_of((part_width,)),
    )
    coming_back = jnp.zeros(images.shape[1:], jnp.bfloat16)
    grads_in = jnp.zeros(images.shape, jnp.float32)
    for step_index in range(micro_count + 1):
        where_from, active, placed = locate(micro_count - step_index - section_index)
        own_grad = lax.dynamic_index_in_dim(cotangent, where_from, 0, keepdims=False)
        entering = jnp.where(
            active, jnp.where(section_index == 1, own_grad, coming_back), jnp.zeros_like(own_grad)
        )
        stream_grad, grad_sums = layer_backward(
            entering, saved_states[micro_count - step_index], params, column, grad_sums
        )
        grads_in = grads_in + placed[:, None, None].astype(jnp.float32) * stream_grad[None]
        if step_index < micro_count:
            coming_back = shifted(stream_grad.astype(jnp.bfloat16), "section", -1)
    flat_sums = member_sum(jnp.concatenate([gradient.reshape(-1) for gradient in grad_sums]))
    unpacked = []
    offset = 0
    for gradient in grad_sums:
        unpacked.append(flat_sums[offset : offset + gradient.size].reshape(gradient.shape))
        offset += gradient.size
    grad_sums = tuple(unpacked)
    return (layer_outputs[None], grads_in[None]) + tuple((gradient[None] for gradient in grad_sums))


def solution(mesh):
    in_specs = (
        P("dp", None, "tensor"),
        P("dp"),
        P("section", None),
        P("section", None),
        P("section", None, None, "tensor"),
        P("section", None, "tensor"),
        P("section", "tensor", None),
        P("section", None),
        P("section", None),
        P("section", None),
        P("section", None, "tensor"),
        P("section", "tensor"),
        P("section", "tensor", None),
        P("section", None),
        P("dp", None, "tensor"),
    )
    out_specs = (
        P("section", "dp", None, "tensor"),
        P("section", "dp", None, "tensor"),
        P("section", "tensor"),
        P("section", "tensor"),
        P("section", None, None, "tensor"),
        P("section", None, "tensor"),
        P("section", "tensor", None),
        P("section", "tensor"),
        P("section", "tensor"),
        P("section", "tensor"),
        P("section", None, "tensor"),
        P("section", "tensor"),
        P("section", "tensor", None),
        P("section", "tensor"),
    )
    return jax.shard_map(shards, mesh=mesh, in_specs=in_specs, out_specs=out_specs, check_vma=False)
```

profile of v0, /device:TPU:1, one launch (start us, length us, event | category | flops | bytes accessed | tf_op | source)
XLA Modules:
  0.0 821.9 jit_solution(293552219122720393)
XLA Ops:
  11.7 13.4 %all-gather = bf16[1,577,768]{1,2,0:T(8,128)(2,1)S(1)} all-gather(bf16[1,577,192]{1,2,0:T(8,128)(2,1)S(1)} %dynamic-slice_select_fusion), channel_id=2, replica_groups=mesh['section'=2,'dp'=16,'tensor'=4] {'tensor'}, dimensions={2}, use_global_device_ids=true | all-gather | bytes 1107840 | tf_op jit(solution)/shard_map/all_gather | solution.py:75
  35.3 4.4 all-to-all-start
  39.7 14.4 %all-to-all-done = bf16[577,4,192]{0,2,1:T(8,128)(2,1)} async-done(((bf16[577,4,192]{0,2,1:T(8,128)(2,1)}), bf16[577,4,192]{0,2,1:T(8,128)(2,1)}, u32[]{:S(2)}, u32[]{:S(2)}) %all-to-all-start) | async-done | bytes 886304 | tf_op jit(solution)/shard_map/all_to_all | solution.py:43
  55.5 11.6 %all_gather.46 = bf16[577,768]{0,1:T(8,128)(2,1)S(1)} all-gather(bf16[577,192]{0,1:T(8,128)(2,1)S(1)} %reduce_sum.651), channel_id=1, replica_groups=mesh['section'=2,'dp'=16,'tensor'=4] {'tensor'}, dimensions={1}, use_global_device_ids=true | all-gather | bytes 1107840 | tf_op jit(solution)/shard_map/all_gather | solution.py:51
  69.1 6.6 multiply_convert_fusion.5
  83.2 13.6 %all-to-all-done.1 = bf16[577,4,192]{0,2,1:T(8,128)(2,1)S(1)} async-done(((bf16[577,4,192]{0,2,1:T(8,128)(2,1)}), bf16[577,4,192]{0,2,1:T(8,128)(2,1)S(1)}, u32[]{:S(2)}, u32[]{:S(2)}) %all-to-all-start.1) | async-done | bytes 886304 | tf_op jit(solution)/shard_map/all_to_all | solution.py:43
  106.2 11.6 %all_gather.47 = bf16[577,768]{0,1:T(8,128)(2,1)S(1)} all-gather(bf16[577,192]{0,1:T(8,128)(2,1)S(1)} %bitcast_select_fusion.3), channel_id=1, replica_groups=mesh['section'=2,'dp'=16,'tensor'=4] {'tensor'}, dimensions={1}, use_global_device_ids=true | all-gather | bytes 1107840 | tf_op jit(solution)/shard_map/all_gather | solution.py:75
  127.2 17.9 %all_to_all.156 = bf16[577,4,192]{0,2,1:T(8,128)(2,1)} all-to-all(bf16[577,4,192]{0,2,1:T(8,128)(2,1)S(1)} %bitcast.295), channel_id=1, replica_groups=mesh['section'=2,'dp'=16,'tensor'=4] {'tensor'}, dimensions={1} | all-to-all | bytes 1772544 | tf_op jit(solution)/shard_map/all_to_all | solution.py:43
  146.5 11.9 %all_gather.48 = bf16[577,768]{0,1:T(8,128)(2,1)S(1)} all-gather(bf16[577,192]{0,1:T(8,128)(2,1)S(1)} %reduce_sum.658), channel_id=1, replica_groups=mesh['section'=2,'dp'=16,'tensor'=4] {'tensor'}, dimensions={1}, use_global_device_ids=true | all-gather | bytes 1107840 | tf_op jit(solution)/shard_map/all_gather | solution.py:51
  160.4 6.6 multiply_convert_fusion.4
  171.2 17.1 %all_to_all.157 = bf16[577,4,192]{0,2,1:T(8,128)(2,1)S(1)} all-to-all(bf16[577,4,192]{0,2,1:T(8,128)(2,1)S(1)} %bitcast.296), channel_id=1, replica_groups=mesh['section'=2,'dp'=16,'tensor'=4] {'tensor'}, dimensions={1} | all-to-all | bytes 1772544 | tf_op jit(solution)/shard_map/all_to_all | solution.py:43
  199.2 11.5 %all_gather.49 = bf16[577,768]{0,1:T(8,128)(2,1)S(1)} all-gather(bf16[577,192]{0,1:T(8,128)(2,1)S(1)} %bitcast_select_fusion.2), channel_id=1, replica_groups=mesh['section'=2,'dp'=16,'tensor'=4] {'tensor'}, dimensions={1}, use_global_device_ids=true | all-gather | bytes 1107840 | tf_op jit(solution)/shard_map/all_gather | solution.py:75
  220.8 4.4 all-to-all-start.4
  226.8 20.1 %all-gather.1 = bf16[1,577,768]{1,2,0:T(8,128)(2,1)} all-gather(bf16[1,577,192]{1,2,0:T(8,128)(2,1)S(1)} %select_select_fusion), channel_id=3, replica_groups=mesh['section'=2,'dp'=16,'tensor'=4] {'tensor'}, dimensions={2}, use_global_device_ids=true | all-gather | bytes 1107840 | tf_op jit(solution)/shard_map/all_gather | solution.py:182
  248.3 11.5 %all_gather.50 = bf16[577,768]{0,1:T(8,128)(2,1)S(1)} all-gather(bf16[577,192]{0,1:T(8,128)(2,1)S(1)} %reduce_sum.665), channel_id=1, replica_groups=mesh['section'=2,'dp'=16,'tensor'=4] {'tensor'}, dimensions={1}, use_global_device_ids=true | all-gather | bytes 1107840 | tf_op jit(solution)/shard_map/all_gather | solution.py:51
  261.9 5.7 multiply_convert_fusion.3
  274.7 4.3 all-to-all-start.6
  281.6 11.9 %all-to-all-done.6 = bf16[577,4,192]{0,2,1:T(8,128)(2,1)} async-done(((bf16[577,4,192]{0,2,1:T(8,128)(2,1)}), bf16[577,4,192]{0,2,1:T(8,128)(2,1)}, u32[]{:S(2)}, u32[]{:S(2)}) %all-to-all-start.6) | async-done | bytes 886304 | tf_op jit(solution)/shard_map/all_to_all | solution.py:43
  295.6 12.1 %all_gather.52 = bf16[577,768]{0,1:T(8,128)(2,1)S(1)} all-gather(bf16[577,192]{0,1:T(8,128)(2,1)} %reduce_sum.669), channel_id=1, replica_groups=mesh['section'=2,'dp'=16,'tensor'=4] {'tensor'}, dimensions={1}, use_global_device_ids=true | all-gather | bytes 1107840 | tf_op jit(solution)/shard_map/all_gather | solution.py:51
  323.7 4.3 all-to-all-start.7
  330.6 4.2 fusion.71
  337.4 5.2 all-to-all-done.7
  344.0 11.3 %all_gather.53 = bf16[577,768]{0,1:T(8,128)(2,1)S(1)} all-gather(bf16[577,192]{0,1:T(8,128)(2,1)S(1)} %reduce_sum.673), channel_id=1, replica_groups=mesh['section'=2,'dp'=16,'tensor'=4] {'tensor'}, dimensions={1}, use_global_device_ids=true | all-gather | bytes 1107840 | tf_op jit(solution)/shard_map/all_gather | solution.py:51
  362.3 6.0 collective-permute-done.2
  369.3 11.5 %all_gather.54 = bf16[577,768]{0,1:T(8,128)(2,1)S(1)} all-gather(bf16[577,192]{0,1:T(8,128)(2,1)S(1)} %fusion.126), channel_id=1, replica_groups=mesh['section'=2,'dp'=16,'tensor'=4] {'tensor'}, dimensions={1}, use_global_device_ids=true | all-gather | bytes 1107840 | tf_op jit(solution)/shard_map/all_gather | solution.py:182
  387.9 4.3 all-to-all-start.8
  401.6 5.2 all-to-all-done.8
  408.9 11.6 %all_gather.55 = bf16[577,768]{0,1:T(8,128)(2,1)S(1)} all-gather(bf16[577,192]{0,1:T(8,128)(2,1)} %reduce_sum.676), channel_id=1, replica_groups=mesh['section'=2,'dp'=16,'tensor'=4] {'tensor'}, dimensions={1}, use_global_device_ids=true | all-gather | bytes 1107840 | tf_op jit(solution)/shard_map/all_gather | solution.py:51
  435.1 4.4 all-to-all-start.9
  446.9 7.1 all-to-all-done.9
  455.4 11.3 %all_gather.56 = bf16[577,768]{0,1:T(8,128)(2,1)S(1)} all-gather(bf16[577,192]{0,1:T(8,128)(2,1)S(1)} %reduce_sum.680), channel_id=1, replica_groups=mesh['section'=2,'dp'=16,'tensor'=4] {'tensor'}, dimensions={1}, use_global_device_ids=true | all-gather | bytes 1107840 | tf_op jit(solution)/shard_map/all_gather | solution.py:51
  473.7 5.7 collective-permute-done.3
  480.4 11.7 %all_gather.57 = bf16[577,768]{0,1:T(8,128)(2,1)S(1)} all-gather(bf16[577,192]{0,1:T(8,128)(2,1)S(1)} %fusion.125), channel_id=1, replica_groups=mesh['section'=2,'dp'=16,'tensor'=4] {'tensor'}, dimensions={1}, use_global_device_ids=true | all-gather | bytes 1107840 | tf_op jit(solution)/shard_map/all_gather | solution.py:182
  498.8 4.3 all-to-all-start.10
  503.1 5.4 add_add_fusion.1
  523.1 11.7 %all_gather.58 = bf16[577,768]{0,1:T(8,128)(2,1)S(1)} all-gather(bf16[577,192]{0,1:T(8,128)(2,1)} %reduce_sum.683), channel_id=1, replica_groups=mesh['section'=2,'dp'=16,'tensor'=4] {'tensor'}, dimensions={1}, use_global_device_ids=true | all-gather | bytes 1107840 | tf_op jit(solution)/shard_map/all_gather | solution.py:51
  549.6 4.4 all-to-all-start.11
  560.2 4.2 add_add_fusion.2
  564.4 4.2 copy.77
  568.6 4.7 reshape.471
  574.7 11.7 %all_gather.59 = bf16[577,768]{0,1:T(8,128)(2,1)S(1)} all-gather(bf16[577,192]{0,1:T(8,128)(2,1)S(1)} %reduce_sum.687), channel_id=1, replica_groups=mesh['section'=2,'dp'=16,'tensor'=4] {'tensor'}, dimensions={1}, use_global_device_ids=true | all-gather | bytes 1107840 | tf_op jit(solution)/shard_map/all_gather | solution.py:51
  592.1 64.9 %concatenate.3 = f32[1771776]{0:T(1024)} concatenate(f32[192]{0:T(256)} %add_add_fusion.9, f32[192]{0:T(256)} %add_add_fusion.8, f32[442368]{0:T(1024)} %reshape.471, f32[384]{0:T(512)S(1)} %add.509, f32[147456]{0:T(1024)} %reshape.472, f32[192]{0:T(256)S(1)} %add_add_fusion.7, f32[192]{0:T(256)} %add_add_fusion.6, f32[192]{0:T(256)} %add_add_fusion.5, f32[589824]{0:T(1024)S(1)} %copy-done.30, ...), dimensions={0} | concatenate | bytes 14174208 | tf_op jit(solution)/shard_map/concatenate | solution.py:378
  661.6 4.5 all-to-all-start.5
  668.2 12.4 %all-to-all-done.5 = bf16[577,4,192]{0,2,1:T(8,128)(2,1)S(1)} async-done(((bf16[577,4,192]{0,2,1:T(8,128)(2,1)}), bf16[577,4,192]{0,2,1:T(8,128)(2,1)S(1)}, u32[]{:S(2)}, u32[]{:S(2)}) %all-to-all-start.5) | async-done | bytes 886304 | tf_op jit(solution)/shard_map/all_to_all | solution.py:43
  684.4 102.6 %all-reduce.2.cloned.1.call-done = f32[1771776]{0:T(1024)} async-done(((f32[1771776]{0:T(1024)}), f32[1771776]{0:T(1024)}) %all-reduce.2.cloned.1.call-update) | async-done | bytes 7087120 | tf_op jit(solution)/shard_map/psum | solution.py:37
  791.8 5.0 fusion.162
  803.0 4.6 broadcast_in_dim_reshape.15
  807.6 4.2 copy.78
  (510 shorter events, 238.9 us)
Async XLA Ops:
  7.2 62.0 %copy-start = (bf16[1,768,768]{2,1,0:T(8,128)(2,1)S(1)}, bf16[1,768,768]{2,1,0:T(8,128)(2,1)}, u32[]{:S(2)}) copy-start(bf16[1,768,768]{2,1,0:T(8,128)(2,1)} %param.25) | copy-start | bytes 3538948
  7.2 18.5 %copy-start.127 = (bf16[1,768,3,192]{1,3,2,0:T(8,128)(2,1)S(1)}, bf16[1,768,3,192]{1,3,2,0:T(8,128)(2,1)}, u32[]{:S(2)}) copy-start(bf16[1,768,3,192]{1,3,2,0:T(8,128)(2,1)} %param.19) | copy-start | bytes 2654212
  25.1 42.0 %copy-start.4 = (bf16[1,577,768]{1,2,0:T(8,128)(2,1)}, bf16[1,577,768]{1,2,0:T(8,128)(2,1)S(1)}, u32[]{:S(2)}) copy-start(bf16[1,577,768]{1,2,0:T(8,128)(2,1)S(1)} %all-gather) | copy-start | bytes 2658820
  33.0 6.7 copy-start.118
  33.0 6.7 copy-start.119
  35.3 18.9 %all-to-all-start = ((bf16[577,4,192]{0,2,1:T(8,128)(2,1)}), bf16[577,4,192]{0,2,1:T(8,128)(2,1)}, u32[]{:S(2)}, u32[]{:S(2)}) async-start(bf16[577,4,192]{0,2,1:T(8,128)(2,1)} %bitcast.293), calls=%async_computation | async-start | bytes 1966080 | tf_op jit(solution)/shard_map/all_to_all | solution.py:43
  68.8 6.9 copy-start.6
  69.1 7.5 copy-start.121
  78.8 18.0 %all-to-all-start.1 = ((bf16[577,4,192]{0,2,1:T(8,128)(2,1)}), bf16[577,4,192]{0,2,1:T(8,128)(2,1)S(1)}, u32[]{:S(2)}, u32[]{:S(2)}) async-start(bf16[577,4,192]{0,2,1:T(8,128)(2,1)} %bitcast.15), calls=%async_computation.1 | async-start | bytes 1966080 | tf_op jit(solution)/shard_map/all_to_all | solution.py:43
  98.2 20.2 %copy-start.78 = (bf16[577,192]{0,1:T(8,128)(2,1)}, bf16[577,192]{0,1:T(8,128)(2,1)S(1)}, u32[]{:S(2)}) copy-start(bf16[577,192]{0,1:T(8,128)(2,1)S(1)} %add_convert_fusion.15) | copy-start | bytes 664708
  98.2 7.0 collective-permute-start
  101.5 16.8 %copy-start.128 = (bf16[1,768,3,192]{1,3,2,0:T(8,128)(2,1)S(1)}, bf16[1,768,3,192]{1,3,2,0:T(8,128)(2,1)}, u32[]{:S(2)}) copy-start(bf16[1,768,3,192]{1,3,2,0:T(8,128)(2,1)} %param.19) | copy-start | bytes 2654212
  160.0 6.9 copy-start.14
  160.4 7.5 copy-start.122
  189.6 21.6 %copy-start.80 = (bf16[577,192]{0,1:T(8,128)(2,1)}, bf16[577,192]{0,1:T(8,128)(2,1)S(1)}, u32[]{:S(2)}) copy-start(bf16[577,192]{0,1:T(8,128)(2,1)S(1)} %add_convert_fusion.12) | copy-start | bytes 664708
  189.6 8.6 %collective-permute-start.1 = (bf16[577,192]{0,1:T(8,128)(2,1)S(1)}, bf16[577,192]{0,1:T(8,128)(2,1)S(1)}, u32[]{:S(2)}, u32[]{:S(2)}) collective-permute-start(bf16[577,192]{0,1:T(8,128)(2,1)S(1)} %add_convert_fusion.12), channel_id=1, source_target_pairs={{0,64},{1,65},{2,66},{3,67},{4,68},{5,69},{6,70},{7,71},{8,72},{9,... | collective-permute-start | bytes 664712 | tf_op jit(solution)/shard_map/ppermute | solution.py:14
  194.4 16.8 %copy-start.129 = (bf16[1,768,3,192]{1,3,2,0:T(8,128)(2,1)S(1)}, bf16[1,768,3,192]{1,3,2,0:T(8,128)(2,1)}, u32[]{:S(2)}) copy-start(bf16[1,768,3,192]{1,3,2,0:T(8,128)(2,1)} %param.19) | copy-start | bytes 2654212
  220.8 26.1 %all-to-all-start.4 = ((bf16[577,4,192]{0,2,1:T(8,128)(2,1)}), bf16[577,4,192]{0,2,1:T(8,128)(2,1)}, u32[]{:S(2)}, u32[]{:S(2)}) async-start(bf16[577,4,192]{0,2,1:T(8,128)(2,1)} %bitcast.292), calls=%async_computation.4 | async-start | bytes 1966080 | tf_op jit(solution)/shard_map/all_to_all | solution.py:43
  274.7 18.8 %all-to-all-start.6 = ((bf16[577,4,192]{0,2,1:T(8,128)(2,1)}), bf16[577,4,192]{0,2,1:T(8,128)(2,1)}, u32[]{:S(2)}, u32[]{:S(2)}) async-start(bf16[577,4,192]{0,2,1:T(8,128)(2,1)} %bitcast.294), calls=%async_computation.6 | async-start | bytes 1966080 | tf_op jit(solution)/shard_map/all_to_all | solution.py:43
  279.0 34.7 %slice-start.4 = ((s8[4485120]{0:T(1024)(128)(4,1)}), s8[290816]{0:T(1024)(128)(4,1)S(1)}, s32[]{:S(2)}) async-start(s8[4485120]{0:T(1024)(128)(4,1)} %bitcast.273), calls=%async_computation.17 | async-start | bytes 581632
  295.6 15.6 %copy-start.17 = (bf16[577,768]{0,1:T(8,128)(2,1)S(1)}, bf16[577,768]{0,1:T(8,128)(2,1)}, u32[]{:S(2)}) copy-start(bf16[577,768]{0,1:T(8,128)(2,1)} %copy-done.16) | copy-start | bytes 2658820
  295.6 15.6 %copy-start.32 = (bf16[1,577,768]{1,2,0:T(8,128)(2,1)S(1)}, bf16[1,577,768]{1,2,0:T(8,128)(2,1)}, u32[]{:S(2)}) copy-start(bf16[1,577,768]{1,2,0:T(8,128)(2,1)} %all-gather.1) | copy-start | bytes 2658820
  323.7 18.8 %all-to-all-start.7 = ((bf16[577,4,192]{0,2,1:T(8,128)(2,1)}), bf16[577,4,192]{0,2,1:T(8,128)(2,1)}, u32[]{:S(2)}, u32[]{:S(2)}) async-start(bf16[577,4,192]{0,2,1:T(8,128)(2,1)} %bitcast.288), calls=%async_computation.7 | async-start | bytes 1966080 | tf_op jit(solution)/shard_map/all_to_all | solution.py:43
  358.7 9.5 %collective-permute-start.2 = (bf16[577,192]{0,1:T(8,128)(2,1)S(1)}, bf16[577,192]{0,1:T(8,128)(2,1)S(1)}, u32[]{:S(2)}, u32[]{:S(2)}) collective-permute-start(bf16[577,192]{0,1:T(8,128)(2,1)S(1)} %get-tuple-element.62), channel_id=1, source_target_pairs={{64,0},{65,1},{66,2},{67,3},{68,4},{69,5},{70,6},{71,7},{72,8},{73... | collective-permute-start | bytes 664712 | tf_op jit(solution)/shard_map/ppermute | solution.py:14
  360.0 20.7 %copy-start.140 = (f32[577,768]{1,0:T(8,128)S(1)}, f32[577,768]{1,0:T(8,128)}, u32[]{:S(2)}) copy-start(f32[577,768]{1,0:T(8,128)} %get-tuple-element.70) | copy-start | bytes 5317636
  360.1 20.7 %copy-start.141 = (f32[577,768]{1,0:T(8,128)S(1)}, f32[577,768]{1,0:T(8,128)}, u32[]{:S(2)}) copy-start(f32[577,768]{1,0:T(8,128)} %get-tuple-element.120) | copy-start | bytes 5317636
  362.3 18.4 %copy-start.124 = (bf16[1,768,768]{2,1,0:T(8,128)(2,1)S(1)}, bf16[1,768,768]{2,1,0:T(8,128)(2,1)}, u32[]{:S(2)}) copy-start(bf16[1,768,768]{2,1,0:T(8,128)(2,1)} %param.27) | copy-start | bytes 3538948
  385.6 8.4 %copy-start.20 = (bf16[577,768]{0,1:T(8,128)(2,1)S(1)}, bf16[577,768]{0,1:T(8,128)(2,1)}, u32[]{:S(2)}) copy-start(bf16[577,768]{0,1:T(8,128)(2,1)} %copy-done.19) | copy-start | bytes 2658820
  387.9 18.9 %all-to-all-start.8 = ((bf16[577,4,192]{0,2,1:T(8,128)(2,1)}), bf16[577,4,192]{0,2,1:T(8,128)(2,1)}, u32[]{:S(2)}, u32[]{:S(2)}) async-start(bf16[577,4,192]{0,2,1:T(8,128)(2,1)} %bitcast.290), calls=%async_computation.8 | async-start | bytes 1966080 | tf_op jit(solution)/shard_map/all_to_all | solution.py:43
  398.9 26.1 %slice-start.2 = ((s8[4485120]{0:T(1024)(128)(4,1)}), s8[290816]{0:T(1024)(128)(4,1)S(1)}, s32[]{:S(2)}) async-start(s8[4485120]{0:T(1024)(128)(4,1)} %bitcast.271), calls=%async_computation.15 | async-start | bytes 581632
  408.9 13.5 %copy-start.35 = (bf16[577,768]{0,1:T(8,128)(2,1)S(1)}, bf16[577,768]{0,1:T(8,128)(2,1)}, u32[]{:S(2)}) copy-start(bf16[577,768]{0,1:T(8,128)(2,1)} %copy-done.33) | copy-start | bytes 2658820
  432.8 6.7 copy-start.36
  435.1 18.9 %all-to-all-start.9 = ((bf16[577,4,192]{0,2,1:T(8,128)(2,1)}), bf16[577,4,192]{0,2,1:T(8,128)(2,1)}, u32[]{:S(2)}, u32[]{:S(2)}) async-start(bf16[577,4,192]{0,2,1:T(8,128)(2,1)} %bitcast.291), calls=%async_computation.9 | async-start | bytes 1966080 | tf_op jit(solution)/shard_map/all_to_all | solution.py:43
  470.1 9.3 %collective-permute-start.3 = (bf16[577,192]{0,1:T(8,128)(2,1)S(1)}, bf16[577,192]{0,1:T(8,128)(2,1)S(1)}, u32[]{:S(2)}, u32[]{:S(2)}) collective-permute-start(bf16[577,192]{0,1:T(8,128)(2,1)S(1)} %get-tuple-element.60), channel_id=1, source_target_pairs={{64,0},{65,1},{66,2},{67,3},{68,4},{69,5},{70,6},{71,7},{72,8},{73... | collective-permute-start | bytes 664712 | tf_op jit(solution)/shard_map/ppermute | solution.py:14
  471.4 20.7 %copy-start.138 = (f32[577,768]{1,0:T(8,128)S(1)}, f32[577,768]{1,0:T(8,128)}, u32[]{:S(2)}) copy-start(f32[577,768]{1,0:T(8,128)} %get-tuple-element.75) | copy-start | bytes 5317636
  471.5 20.7 %copy-start.139 = (f32[577,768]{1,0:T(8,128)S(1)}, f32[577,768]{1,0:T(8,128)}, u32[]{:S(2)}) copy-start(f32[577,768]{1,0:T(8,128)} %get-tuple-element.117) | copy-start | bytes 5317636
  473.7 18.4 %copy-start.125 = (bf16[1,768,768]{2,1,0:T(8,128)(2,1)S(1)}, bf16[1,768,768]{2,1,0:T(8,128)(2,1)}, u32[]{:S(2)}) copy-start(bf16[1,768,768]{2,1,0:T(8,128)(2,1)} %param.27) | copy-start | bytes 3538948
  496.5 6.7 copy-start.7
  498.8 22.2 %all-to-all-start.10 = ((bf16[577,4,192]{0,2,1:T(8,128)(2,1)}), bf16[577,4,192]{0,2,1:T(8,128)(2,1)}, u32[]{:S(2)}, u32[]{:S(2)}) async-start(bf16[577,4,192]{0,2,1:T(8,128)(2,1)} %bitcast.289), calls=%async_computation.10 | async-start | bytes 1966080 | tf_op jit(solution)/shard_map/all_to_all | solution.py:43
  515.9 23.3 %slice-start = ((s8[4485120]{0:T(1024)(128)(4,1)}), s8[290816]{0:T(1024)(128)(4,1)S(1)}, s32[]{:S(2)}) async-start(s8[4485120]{0:T(1024)(128)(4,1)} %bitcast.269), calls=%async_computation.13 | async-start | bytes 581632
  547.2 6.7 copy-start.13
  547.2 6.7 copy-start.56
  549.6 23.7 %all-to-all-start.11 = ((bf16[577,4,192]{0,2,1:T(8,128)(2,1)}), bf16[577,4,192]{0,2,1:T(8,128)(2,1)}, u32[]{:S(2)}, u32[]{:S(2)}) async-start(bf16[577,4,192]{0,2,1:T(8,128)(2,1)} %bitcast.287), calls=%async_computation.11 | async-start | bytes 1966080 | tf_op jit(solution)/shard_map/all_to_all | solution.py:43
  554.0 233.1 %all-reduce.2.cloned.1.call-start = ((), (), s32[]{:S(2)}) async-start(), calls=%async_computation.12 | async-start | bytes 14180352 | tf_op jit(solution)/shard_map/psum | solution.py:37
  661.6 20.2 %copy-start.79 = (bf16[577,192]{0,1:T(8,128)(2,1)S(1)}, bf16[577,192]{0,1:T(8,128)(2,1)}, u32[]{:S(2)}) copy-start(bf16[577,192]{0,1:T(8,128)(2,1)} %copy-done.78) | copy-start | bytes 664708
  661.6 18.9 %all-to-all-start.5 = ((bf16[577,4,192]{0,2,1:T(8,128)(2,1)}), bf16[577,4,192]{0,2,1:T(8,128)(2,1)S(1)}, u32[]{:S(2)}, u32[]{:S(2)}) async-start(bf16[577,4,192]{0,2,1:T(8,128)(2,1)} %bitcast.38), calls=%async_computation.5 | async-start | bytes 1966080 | tf_op jit(solution)/shard_map/all_to_all | solution.py:43
  668.1 14.9 %copy-start.75 = (f32[577,192]{0,1:T(8,128)S(1)}, f32[577,192]{0,1:T(8,128)}, u32[]{:S(2)}) copy-start(f32[577,192]{0,1:T(8,128)} %get-tuple-element.63) | copy-start | bytes 1329412
  668.1 14.9 %copy-start.76 = (f32[577,192]{0,1:T(8,128)S(1)}, f32[577,192]{0,1:T(8,128)}, u32[]{:S(2)}) copy-start(f32[577,192]{0,1:T(8,128)} %get-tuple-element.61) | copy-start | bytes 1329412
  (115 other events, 289.3 us)
Sparse Core Ops, SparseCore 0:
  657.1 129.8 all-reduce.1
where the time goes:
time: 833 us; the launch traced here: 822 us
  blocking collectives  219 us (26%)
  waiting for transfers between devices  192 us (23%)
  local copies, waits for them, and re-layouts  157 us (19%)
  matrix products  99.9 us (12%)
  other arithmetic  82 us (10%)
  starting transfers between devices  52.3 us (6%)
  between operations  20 us (2%)
    all_gather x9, blocking collectives, tensor_sum(): lax.all_gather(summed.astype(jnp.bfloat16), 'tensor', axis=1, tiled=True)  105 us
    psum x1, waiting for transfers between devices, member_sum(): return lax.psum(gradients, 'dp')  103 us
    all_to_all x10, waiting for transfers between devices, tensor_scatter_sum(): lax.all_to_all(partial_value.astype(jnp.bfloat16), 'tensor', 1, 0, tiled=...  69.8 us
    concatenate x1, local copies, waits for them, and re-layouts, shards(): jnp.concatenate([gradient.reshape(-1) for gradient in grad_sums])  64.9 us
    all_gather x3, blocking collectives, layer_backward(): grad_full_bf16 = lax.all_gather(grad_part, 'tensor', axis=1, tiled=True)  43.2 us
    all_to_all x10, starting transfers between devices, tensor_scatter_sum(): lax.all_to_all(partial_value.astype(jnp.bfloat16), 'tensor', 1, 0, tiled=...  42.9 us
    all_gather x3, blocking collectives, layer_forward(): lax.all_gather(partial_residual, 'tensor', axis=1, tiled=True)  36.5 us
    dot_general x12, matrix products, contract_rows(): lax.dot_general(left_side, right_side, (((0,), (0,)), ((), ())), preferre...  35.1 us
  transfers between devices with their start and end apart: 15, of which 12 were waited for; matrix products, arithmetic and copies ran while one was open for 10% of the time, Pallas kernels for 0%

commit v1 on v0

--- a/solution.py
+++ b/solution.py
@@ -3,9 +3,19 @@
 import jax.numpy as jnp
 from jax import lax
 from jax.sharding import PartitionSpec as P
+from jax.lax import all_to_all, axis_size
 
 HD = 64
 epsilon = 1e-06
+direct_works = lambda work_x: jnp.concatenate(
+    all_to_all(
+        jnp.stack([work_x for _ in range(axis_size("tensor"))], 0),
+        axis_name="tensor",
+        split_axis=0,
+        concat_axis=0,
+    ),
+    1,
+)
 
 
 def shifted(block, axis, distance):
@@ -179,7 +189,7 @@
     def local_cols(matrix):
         return lax.dynamic_slice_in_dim(matrix, column, part_width, 1)
 
-    grad_full_bf16 = lax.all_gather(grad_part, "tensor", axis=1, tiled=True)
+    grad_full_bf16 = direct_works(grad_part)
     grad_full = grad_full_bf16.astype(jnp.float32)
     down_grad = contract_rows(hidden, grad_full_bf16)
     down_add_grad = jnp.sum(local_cols(grad_full), axis=0)

time: 833 us -> 863 us (1.036)
  waiting for transfers between devices: 192 us -> 206 us
    all_gather x3 -> x0, blocking collectives: 43.2 us -> none  [layer_backward(): grad_full_bf16 = lax.all_gather(grad_part, 'tensor', axis=1, tiled=True)]
    all_to_all x2 -> x4, blocking collectives: 35 us -> 73 us  [tensor_scatter_sum(): lax.all_to_all(partial_value.astype(jnp.bfloat16), 'tensor', 1, 0, tiled=...]
    all_to_all x0 -> x3, waiting for transfers between devices: none -> 20.5 us  [all_to_all(jnp.stack([work_x for _ in range(axis_size('tensor'))], 0), ax...]
    all_to_all x0 -> x3, starting transfers between devices: none -> 15.2 us  [all_to_all(jnp.stack([work_x for _ in range(axis_size('tensor'))], 0), ax...]
    all_to_all x10 -> x8, starting transfers between devices: 42.9 us -> 35.2 us  [tensor_scatter_sum(): lax.all_to_all(partial_value.astype(jnp.bfloat16), 'tensor', 1, 0, tiled=...]
    all_to_all x10 -> x8, waiting for transfers between devices: 69.8 us -> 63.6 us  [tensor_scatter_sum(): lax.all_to_all(partial_value.astype(jnp.bfloat16), 'tensor', 1, 0, tiled=...]
    unnamed x297 -> x249, local copies, waits for them, and re-layouts: 25.3 us -> 24.3 us
  transfers between devices with their start and end apart: 15 -> 16, of which waited for: 12 -> 13; matrix products, arithmetic and copies ran while one was open for 10% -> 11% of each run, Pallas kernels for 0% -> 0%
where the time goes in v1:
time: 863 us; the launch traced here: 852 us
  blocking collectives  222 us (26%)
  waiting for transfers between devices  206 us (24%)
  local copies, waits for them, and re-layouts  154 us (18%)
  matrix products  108 us (13%)
  other arithmetic  82.2 us (10%)
  starting transfers between devices  59.8 us (7%)
  between operations  19.9 us (2%)
    all_gather x9, blocking collectives, tensor_sum(): lax.all_gather(summed.astype(jnp.bfloat16), 'tensor', axis=1, tiled=True)  113 us
    psum x1, waiting for transfers between devices, member_sum(): return lax.psum(gradients, 'dp')  103 us
    all_to_all x4, blocking collectives, tensor_scatter_sum(): lax.all_to_all(partial_value.astype(jnp.bfloat16), 'tensor', 1, 0, tiled=...  73 us
    all_to_all x8, waiting for transfers between devices, tensor_scatter_sum(): lax.all_to_all(partial_value.astype(jnp.bfloat16), 'tensor', 1, 0, tiled=...  63.6 us
    concatenate x1, local copies, waits for them, and re-layouts, shards(): jnp.concatenate([gradient.reshape(-1) for gradient in grad_sums])  62.2 us
    all_gather x3, blocking collectives, layer_forward(): lax.all_gather(partial_residual, 'tensor', axis=1, tiled=True)  36.5 us
    dot_general x12, matrix products, contract_rows(): lax.dot_general(left_side, right_side, (((0,), (0,)), ((), ())), preferre...  36.3 us
    all_to_all x8, starting transfers between devices, tensor_scatter_sum(): lax.all_to_all(partial_value.astype(jnp.bfloat16), 'tensor', 1, 0, tiled=...  35.2 us
  transfers between devices with their start and end apart: 16, of which 13 were waited for; matrix products, arithmetic and copies ran while one was open for 11% of the time, Pallas kernels for 0%

profile of v1, /device:TPU:1, one launch (start us, length us, event | category | flops | bytes accessed | tf_op | source)
XLA Modules:
  0.0 852.0 jit_solution(11705163494429059157)
XLA Ops:
  11.7 13.4 %all-gather = bf16[1,577,768]{1,2,0:T(8,128)(2,1)S(1)} all-gather(bf16[1,577,192]{1,2,0:T(8,128)(2,1)S(1)} %dynamic-slice_select_fusion), channel_id=2, replica_groups=mesh['section'=2,'dp'=16,'tensor'=4] {'tensor'}, dimensions={2}, use_global_device_ids=true | all-gather | bytes 1107840 | tf_op jit(solution)/shard_map/all_gather | solution.py:85
  38.2 14.3 %all-to-all-done = bf16[577,4,192]{0,2,1:T(8,128)(2,1)S(1)} async-done(((bf16[577,4,192]{0,2,1:T(8,128)(2,1)}), bf16[577,4,192]{0,2,1:T(8,128)(2,1)S(1)}, u32[]{:S(2)}, u32[]{:S(2)}) %all-to-all-start) | async-done | bytes 886304 | tf_op jit(solution)/shard_map/all_to_all | solution.py:53
  53.4 11.7 %all_gather.37 = bf16[577,768]{0,1:T(8,128)(2,1)S(1)} all-gather(bf16[577,192]{0,1:T(8,128)(2,1)} %reduce_sum.651), channel_id=1, replica_groups=mesh['section'=2,'dp'=16,'tensor'=4] {'tensor'}, dimensions={1}, use_global_device_ids=true | all-gather | bytes 1107840 | tf_op jit(solution)/shard_map/all_gather | solution.py:61
  67.1 6.5 multiply_convert_fusion.5
  80.2 13.6 %all-to-all-done.1 = bf16[577,4,192]{0,2,1:T(8,128)(2,1)S(1)} async-done(((bf16[577,4,192]{0,2,1:T(8,128)(2,1)}), bf16[577,4,192]{0,2,1:T(8,128)(2,1)S(1)}, u32[]{:S(2)}, u32[]{:S(2)}) %all-to-all-start.1) | async-done | bytes 886304 | tf_op jit(solution)/shard_map/all_to_all | solution.py:53
  103.2 11.5 %all_gather.38 = bf16[577,768]{0,1:T(8,128)(2,1)S(1)} all-gather(bf16[577,192]{0,1:T(8,128)(2,1)S(1)} %bitcast_select_fusion.3), channel_id=1, replica_groups=mesh['section'=2,'dp'=16,'tensor'=4] {'tensor'}, dimensions={1}, use_global_device_ids=true | all-gather | bytes 1107840 | tf_op jit(solution)/shard_map/all_gather | solution.py:85
  124.0 17.9 %all_to_all.171 = bf16[577,4,192]{0,2,1:T(8,128)(2,1)} all-to-all(bf16[577,4,192]{0,2,1:T(8,128)(2,1)S(1)} %bitcast.297), channel_id=1, replica_groups=mesh['section'=2,'dp'=16,'tensor'=4] {'tensor'}, dimensions={1} | all-to-all | bytes 1772544 | tf_op jit(solution)/shard_map/all_to_all | solution.py:53
  143.3 11.5 %all_gather.39 = bf16[577,768]{0,1:T(8,128)(2,1)S(1)} all-gather(bf16[577,192]{0,1:T(8,128)(2,1)S(1)} %reduce_sum.658), channel_id=1, replica_groups=mesh['section'=2,'dp'=16,'tensor'=4] {'tensor'}, dimensions={1}, use_global_device_ids=true | all-gather | bytes 1107840 | tf_op jit(solution)/shard_map/all_gather | solution.py:61
  156.9 6.6 multiply_convert_fusion.4
  167.8 17.1 %all_to_all.172 = bf16[577,4,192]{0,2,1:T(8,128)(2,1)S(1)} all-to-all(bf16[577,4,192]{0,2,1:T(8,128)(2,1)S(1)} %bitcast.298), channel_id=1, replica_groups=mesh['section'=2,'dp'=16,'tensor'=4] {'tensor'}, dimensions={1} | all-to-all | bytes 1772544 | tf_op jit(solution)/shard_map/all_to_all | solution.py:53
  195.8 11.6 %all_gather.40 = bf16[577,768]{0,1:T(8,128)(2,1)S(1)} all-gather(bf16[577,192]{0,1:T(8,128)(2,1)S(1)} %bitcast_select_fusion.2), channel_id=1, replica_groups=mesh['section'=2,'dp'=16,'tensor'=4] {'tensor'}, dimensions={1}, use_global_device_ids=true | all-gather | bytes 1107840 | tf_op jit(solution)/shard_map/all_gather | solution.py:85
  217.4 4.4 all-to-all-start.4
  223.4 12.9 %all-to-all-done.4 = bf16[577,4,192]{0,2,1:T(8,128)(2,1)} async-done(((bf16[577,4,192]{0,2,1:T(8,128)(2,1)}), bf16[577,4,192]{0,2,1:T(8,128)(2,1)}, u32[]{:S(2)}, u32[]{:S(2)}) %all-to-all-start.4) | async-done | bytes 886304 | tf_op jit(solution)/shard_map/all_to_all | solution.py:53
  237.3 5.1 all-to-all-start.6
  243.8 19.9 %all_gather.41 = bf16[577,768]{0,1:T(8,128)(2,1)S(1)} all-gather(bf16[577,192]{0,1:T(8,128)(2,1)S(1)} %reduce_sum.665), channel_id=1, replica_groups=mesh['section'=2,'dp'=16,'tensor'=4] {'tensor'}, dimensions={1}, use_global_device_ids=true | all-gather | bytes 1107840 | tf_op jit(solution)/shard_map/all_gather | solution.py:61
  266.3 6.8 multiply_convert_fusion.3
  273.1 4.7 convert_reduce_fusion.11
  282.8 19.1 %all_to_all.173 = bf16[577,4,192]{0,2,1:T(8,128)(2,1)} all-to-all(bf16[577,4,192]{0,2,1:T(8,128)(2,1)} %bitcast.299), channel_id=1, replica_groups=mesh['section'=2,'dp'=16,'tensor'=4] {'tensor'}, dimensions={1} | all-to-all | bytes 1772544 | tf_op jit(solution)/shard_map/all_to_all | solution.py:53
  304.0 11.8 %all_gather.42 = bf16[577,768]{0,1:T(8,128)(2,1)S(1)} all-gather(bf16[577,192]{0,1:T(8,128)(2,1)} %reduce_sum.669), channel_id=1, replica_groups=mesh['section'=2,'dp'=16,'tensor'=4] {'tensor'}, dimensions={1}, use_global_device_ids=true | all-gather | bytes 1107840 | tf_op jit(solution)/shard_map/all_gather | solution.py:61
  333.0 19.0 %all_to_all.174 = bf16[577,4,192]{0,2,1:T(8,128)(2,1)} all-to-all(bf16[577,4,192]{0,2,1:T(8,128)(2,1)} %bitcast.300), channel_id=1, replica_groups=mesh['section'=2,'dp'=16,'tensor'=4] {'tensor'}, dimensions={1} | all-to-all | bytes 1772544 | tf_op jit(solution)/shard_map/all_to_all | solution.py:53
  353.4 11.3 %all_gather.43 = bf16[577,768]{0,1:T(8,128)(2,1)S(1)} all-gather(bf16[577,192]{0,1:T(8,128)(2,1)S(1)} %reduce_sum.673), channel_id=1, replica_groups=mesh['section'=2,'dp'=16,'tensor'=4] {'tensor'}, dimensions={1}, use_global_device_ids=true | all-gather | bytes 1107840 | tf_op jit(solution)/shard_map/all_gather | solution.py:61
  369.4 7.7 collective-permute-done.2
  379.2 5.0 all-to-all-start.9
  386.4 12.4 %all-to-all-done.9 = bf16[4,577,192]{1,2,0:T(8,128)(2,1)} async-done(((bf16[4,577,192]{1,2,0:T(8,128)(2,1)}), bf16[4,577,192]{1,2,0:T(8,128)(2,1)}, u32[]{:S(2)}, u32[]{:S(2)}) %all-to-all-start.9) | async-done | bytes 886304 | tf_op jit(solution)/shard_map/all_to_all | solution.py:11
  398.8 4.7 convert_reduce_fusion.10
  408.5 5.3 all-to-all-start.10
  413.8 4.2 fusion.164
  423.0 5.3 all-to-all-done.10
  430.4 11.5 %all_gather.44 = bf16[577,768]{0,1:T(8,128)(2,1)S(1)} all-gather(bf16[577,192]{0,1:T(8,128)(2,1)} %reduce_sum.676), channel_id=1, replica_groups=mesh['section'=2,'dp'=16,'tensor'=4] {'tensor'}, dimensions={1}, use_global_device_ids=true | all-gather | bytes 1107840 | tf_op jit(solution)/shard_map/all_gather | solution.py:61
  458.0 4.8 all-to-all-start.11
  472.2 5.1 all-to-all-done.11
  478.7 11.3 %all_gather.45 = bf16[577,768]{0,1:T(8,128)(2,1)S(1)} all-gather(bf16[577,192]{0,1:T(8,128)(2,1)S(1)} %reduce_sum.680), channel_id=1, replica_groups=mesh['section'=2,'dp'=16,'tensor'=4] {'tensor'}, dimensions={1}, use_global_device_ids=true | all-gather | bytes 1107840 | tf_op jit(solution)/shard_map/all_gather | solution.py:61
  504.1 5.2 all-to-all-start.12
  515.6 8.1 all-to-all-done.12
  531.0 4.4 all-to-all-start.13
  535.4 5.4 add_add_fusion.1
  556.5 11.9 %all_gather.46 = bf16[577,768]{0,1:T(8,128)(2,1)S(1)} all-gather(bf16[577,192]{0,1:T(8,128)(2,1)} %reduce_sum.683), channel_id=1, replica_groups=mesh['section'=2,'dp'=16,'tensor'=4] {'tensor'}, dimensions={1}, use_global_device_ids=true | all-gather | bytes 1107840 | tf_op jit(solution)/shard_map/all_gather | solution.py:61
  584.8 4.4 all-to-all-start.14
  595.4 4.3 add_add_fusion.2
  599.6 4.2 copy.77
  603.9 4.7 reshape.494
  610.0 11.8 %all_gather.47 = bf16[577,768]{0,1:T(8,128)(2,1)S(1)} all-gather(bf16[577,192]{0,1:T(8,128)(2,1)S(1)} %reduce_sum.687), channel_id=1, replica_groups=mesh['section'=2,'dp'=16,'tensor'=4] {'tensor'}, dimensions={1}, use_global_device_ids=true | all-gather | bytes 1107840 | tf_op jit(solution)/shard_map/all_gather | solution.py:61
  625.1 62.2 %concatenate.3 = f32[1771776]{0:T(1024)} concatenate(f32[192]{0:T(256)S(1)} %add_add_fusion.9, f32[192]{0:T(256)S(1)} %add_add_fusion.8, f32[442368]{0:T(1024)S(1)} %copy-done.28, f32[384]{0:T(512)S(1)} %add.509, f32[147456]{0:T(1024)} %reshape.495, f32[192]{0:T(256)S(1)} %add_add_fusion.7, f32[192]{0:T(256)S(1)} %add_add_fusion.6, f32[192]{0:T(256)S(1)} %add_add_fusion.5, ...), dimensions={0} | concatenate | bytes 14174208 | tf_op jit(solution)/shard_map/concatenate | solution.py:388
  691.9 4.5 all-to-all-start.5
  698.4 12.4 %all-to-all-done.5 = bf16[577,4,192]{0,2,1:T(8,128)(2,1)S(1)} async-done(((bf16[577,4,192]{0,2,1:T(8,128)(2,1)}), bf16[577,4,192]{0,2,1:T(8,128)(2,1)S(1)}, u32[]{:S(2)}, u32[]{:S(2)}) %all-to-all-start.5) | async-done | bytes 886304 | tf_op jit(solution)/shard_map/all_to_all | solution.py:53
  714.7 102.6 %all-reduce.2.cloned.1.call-done = f32[1771776]{0:T(1024)} async-done(((f32[1771776]{0:T(1024)}), f32[1771776]{0:T(1024)}) %all-reduce.2.cloned.1.call-update) | async-done | bytes 7087120 | tf_op jit(solution)/shard_map/psum | solution.py:47
  822.1 5.8 fusion.159
  835.9 4.2 copy.78
  (466 shorter events, 248.3 us)
Async XLA Ops:
  7.2 59.9 %copy-start = (bf16[1,768,768]{2,1,0:T(8,128)(2,1)S(1)}, bf16[1,768,768]{2,1,0:T(8,128)(2,1)}, u32[]{:S(2)}) copy-start(bf16[1,768,768]{2,1,0:T(8,128)(2,1)} %param.25) | copy-start | bytes 3538948
  10.7 15.0 %copy-start.105 = (bf16[1,768,3,192]{1,3,2,0:T(8,128)(2,1)S(1)}, bf16[1,768,3,192]{1,3,2,0:T(8,128)(2,1)}, u32[]{:S(2)}) copy-start(bf16[1,768,3,192]{1,3,2,0:T(8,128)(2,1)} %param.19) | copy-start | bytes 2654212
  25.1 40.0 %copy-start.4 = (bf16[1,577,768]{1,2,0:T(8,128)(2,1)}, bf16[1,577,768]{1,2,0:T(8,128)(2,1)S(1)}, u32[]{:S(2)}) copy-start(bf16[1,577,768]{1,2,0:T(8,128)(2,1)S(1)} %all-gather) | copy-start | bytes 2658820
  32.8 5.4 copy-start.100
  32.8 5.4 copy-start.101
  34.1 18.4 %all-to-all-start = ((bf16[577,4,192]{0,2,1:T(8,128)(2,1)}), bf16[577,4,192]{0,2,1:T(8,128)(2,1)S(1)}, u32[]{:S(2)}, u32[]{:S(2)}) async-start(bf16[577,4,192]{0,2,1:T(8,128)(2,1)} %bitcast.12), calls=%async_computation | async-start | bytes 1966080 | tf_op jit(solution)/shard_map/all_to_all | solution.py:53
  38.2 360.6 %copy-start.93 = (f32[768]{0:T(1024)}, f32[768]{0:T(1024)S(1)}, u32[]{:S(2)}) copy-start(f32[768]{0:T(1024)S(1)} %reduce.44) | copy-start | bytes 9220
  66.8 6.8 copy-start.6
  67.1 6.5 copy-start.103
  75.8 18.0 %all-to-all-start.1 = ((bf16[577,4,192]{0,2,1:T(8,128)(2,1)}), bf16[577,4,192]{0,2,1:T(8,128)(2,1)S(1)}, u32[]{:S(2)}, u32[]{:S(2)}) async-start(bf16[577,4,192]{0,2,1:T(8,128)(2,1)} %bitcast.15), calls=%async_computation.1 | async-start | bytes 1966080 | tf_op jit(solution)/shard_map/all_to_all | solution.py:53
  95.1 20.0 %copy-start.68 = (bf16[577,192]{0,1:T(8,128)(2,1)}, bf16[577,192]{0,1:T(8,128)(2,1)S(1)}, u32[]{:S(2)}) copy-start(bf16[577,192]{0,1:T(8,128)(2,1)S(1)} %add_convert_fusion.15) | copy-start | bytes 664708
  95.2 7.0 collective-permute-start
  98.5 16.7 %copy-start.106 = (bf16[1,768,3,192]{1,3,2,0:T(8,128)(2,1)S(1)}, bf16[1,768,3,192]{1,3,2,0:T(8,128)(2,1)}, u32[]{:S(2)}) copy-start(bf16[1,768,3,192]{1,3,2,0:T(8,128)(2,1)} %param.19) | copy-start | bytes 2654212
  156.5 7.0 copy-start.14
  156.9 7.6 copy-start.104
  186.2 8.6 %copy-start.70 = (bf16[577,192]{0,1:T(8,128)(2,1)}, bf16[577,192]{0,1:T(8,128)(2,1)S(1)}, u32[]{:S(2)}) copy-start(bf16[577,192]{0,1:T(8,128)(2,1)S(1)} %add_convert_fusion.12) | copy-start | bytes 664708
  186.2 8.6 %collective-permute-start.1 = (bf16[577,192]{0,1:T(8,128)(2,1)S(1)}, bf16[577,192]{0,1:T(8,128)(2,1)S(1)}, u32[]{:S(2)}, u32[]{:S(2)}) collective-permute-start(bf16[577,192]{0,1:T(8,128)(2,1)S(1)} %add_convert_fusion.12), channel_id=1, source_target_pairs={{0,64},{1,65},{2,66},{3,67},{4,68},{5,69},{6,70},{7,71},{8,72},{9,... | collective-permute-start | bytes 664712 | tf_op jit(solution)/shard_map/ppermute | solution.py:24
  190.9 16.9 %copy-start.107 = (bf16[1,768,3,192]{1,3,2,0:T(8,128)(2,1)S(1)}, bf16[1,768,3,192]{1,3,2,0:T(8,128)(2,1)}, u32[]{:S(2)}) copy-start(bf16[1,768,3,192]{1,3,2,0:T(8,128)(2,1)} %param.19) | copy-start | bytes 2654212
  217.4 18.9 %all-to-all-start.4 = ((bf16[577,4,192]{0,2,1:T(8,128)(2,1)}), bf16[577,4,192]{0,2,1:T(8,128)(2,1)}, u32[]{:S(2)}, u32[]{:S(2)}) async-start(bf16[577,4,192]{0,2,1:T(8,128)(2,1)} %bitcast.295), calls=%async_computation.4 | async-start | bytes 1966080 | tf_op jit(solution)/shard_map/all_to_all | solution.py:53
  237.3 35.8 %all-to-all-start.6 = ((bf16[4,577,192]{1,2,0:T(8,128)(2,1)}), bf16[4,577,192]{1,2,0:T(8,128)(2,1)}, u32[]{:S(2)}, u32[]{:S(2)}) async-start(bf16[4,577,192]{1,2,0:T(8,128)(2,1)} %stack.60), calls=%async_computation.6 | async-start | bytes 1966080 | tf_op jit(solution)/shard_map/all_to_all | solution.py:11
  282.8 40.2 %slice-start.4 = ((s8[4485120]{0:T(1024)(128)(4,1)}), s8[290816]{0:T(1024)(128)(4,1)S(1)}, s32[]{:S(2)}) async-start(s8[4485120]{0:T(1024)(128)(4,1)} %bitcast.279), calls=%async_computation.20 | async-start | bytes 581632
  304.0 15.3 %copy-start.17 = (bf16[577,768]{0,1:T(8,128)(2,1)S(1)}, bf16[577,768]{0,1:T(8,128)(2,1)}, u32[]{:S(2)}) copy-start(bf16[577,768]{0,1:T(8,128)(2,1)} %copy-done.16) | copy-start | bytes 2658820
  315.8 7.2 slice-start.5
  367.5 9.6 %collective-permute-start.2 = (bf16[577,192]{0,1:T(8,128)(2,1)S(1)}, bf16[577,192]{0,1:T(8,128)(2,1)}, u32[]{:S(2)}, u32[]{:S(2)}) collective-permute-start(bf16[577,192]{0,1:T(8,128)(2,1)S(1)} %get-tuple-element.62), channel_id=1, source_target_pairs={{64,0},{65,1},{66,2},{67,3},{68,4},{69,5},{70,6},{71,7},{72,8},{73... | collective-permute-start | bytes 664712 | tf_op jit(solution)/shard_map/ppermute | solution.py:24
  379.2 19.5 %all-to-all-start.9 = ((bf16[4,577,192]{1,2,0:T(8,128)(2,1)}), bf16[4,577,192]{1,2,0:T(8,128)(2,1)}, u32[]{:S(2)}, u32[]{:S(2)}) async-start(bf16[4,577,192]{1,2,0:T(8,128)(2,1)} %stack.62), calls=%async_computation.9 | async-start | bytes 1966080 | tf_op jit(solution)/shard_map/all_to_all | solution.py:11
  408.5 19.8 %all-to-all-start.10 = ((bf16[577,4,192]{0,2,1:T(8,128)(2,1)}), bf16[577,4,192]{0,2,1:T(8,128)(2,1)}, u32[]{:S(2)}, u32[]{:S(2)}) async-start(bf16[577,4,192]{0,2,1:T(8,128)(2,1)} %bitcast.296), calls=%async_computation.10 | async-start | bytes 1966080 | tf_op jit(solution)/shard_map/all_to_all | solution.py:53
  420.7 27.3 %slice-start.2 = ((s8[4485120]{0:T(1024)(128)(4,1)}), s8[290816]{0:T(1024)(128)(4,1)S(1)}, s32[]{:S(2)}) async-start(s8[4485120]{0:T(1024)(128)(4,1)} %bitcast.277), calls=%async_computation.18 | async-start | bytes 581632
  423.0 18.9 %copy-start.15 = (bf16[577,768]{0,1:T(8,128)(2,1)S(1)}, bf16[577,768]{0,1:T(8,128)(2,1)}, u32[]{:S(2)}) copy-start(bf16[577,768]{0,1:T(8,128)(2,1)} %copy-done.14) | copy-start | bytes 2658820
  441.9 6.1 slice-start.3
  458.0 19.2 %all-to-all-start.11 = ((bf16[577,4,192]{0,2,1:T(8,128)(2,1)}), bf16[577,4,192]{0,2,1:T(8,128)(2,1)}, u32[]{:S(2)}, u32[]{:S(2)}) async-start(bf16[577,4,192]{0,2,1:T(8,128)(2,1)} %bitcast.294), calls=%async_computation.11 | async-start | bytes 1966080 | tf_op jit(solution)/shard_map/all_to_all | solution.py:53
  492.8 9.3 %collective-permute-start.3 = (bf16[577,192]{0,1:T(8,128)(2,1)S(1)}, bf16[577,192]{0,1:T(8,128)(2,1)S(1)}, u32[]{:S(2)}, u32[]{:S(2)}) collective-permute-start(bf16[577,192]{0,1:T(8,128)(2,1)S(1)} %get-tuple-element.60), channel_id=1, source_target_pairs={{64,0},{65,1},{66,2},{67,3},{68,4},{69,5},{70,6},{71,7},{72,8},{73... | collective-permute-start | bytes 664712 | tf_op jit(solution)/shard_map/ppermute | solution.py:24
  503.0 7.4 copy-start.21
  504.1 19.7 %all-to-all-start.12 = ((bf16[4,577,192]{1,2,0:T(8,128)(2,1)}), bf16[4,577,192]{1,2,0:T(8,128)(2,1)}, u32[]{:S(2)}, u32[]{:S(2)}) async-start(bf16[4,577,192]{1,2,0:T(8,128)(2,1)} %stack.64), calls=%async_computation.12 | async-start | bytes 1966080 | tf_op jit(solution)/shard_map/all_to_all | solution.py:11
  514.3 9.4 %copy-start.94 = (f32[768]{0:T(1024)S(1)}, f32[768]{0:T(1024)}, u32[]{:S(2)}) copy-start(f32[768]{0:T(1024)} %copy-done.93) | copy-start | bytes 9220
  529.7 5.7 copy-start.7
  531.0 24.5 %all-to-all-start.13 = ((bf16[577,4,192]{0,2,1:T(8,128)(2,1)}), bf16[577,4,192]{0,2,1:T(8,128)(2,1)S(1)}, u32[]{:S(2)}, u32[]{:S(2)}) async-start(bf16[577,4,192]{0,2,1:T(8,128)(2,1)} %bitcast.71), calls=%async_computation.13 | async-start | bytes 1966080 | tf_op jit(solution)/shard_map/all_to_all | solution.py:53
  535.4 5.4 copy-start.42
  535.4 5.4 copy-start.85
  550.6 23.9 %slice-start = ((s8[4485120]{0:T(1024)(128)(4,1)}), s8[290816]{0:T(1024)(128)(4,1)S(1)}, s32[]{:S(2)}) async-start(s8[4485120]{0:T(1024)(128)(4,1)} %bitcast.275), calls=%async_computation.16 | async-start | bytes 581632
  568.4 6.1 slice-start.1
  582.5 6.7 copy-start.13
  582.5 6.7 copy-start.48
  584.8 23.7 %all-to-all-start.14 = ((bf16[577,4,192]{0,2,1:T(8,128)(2,1)}), bf16[577,4,192]{0,2,1:T(8,128)(2,1)}, u32[]{:S(2)}, u32[]{:S(2)}) async-start(bf16[577,4,192]{0,2,1:T(8,128)(2,1)} %bitcast.293), calls=%async_computation.14 | async-start | bytes 1966080 | tf_op jit(solution)/shard_map/all_to_all | solution.py:53
  589.2 228.2 %all-reduce.2.cloned.1.call-start = ((), (), s32[]{:S(2)}) async-start(), calls=%async_computation.15 | async-start | bytes 14180352 | tf_op jit(solution)/shard_map/psum | solution.py:47
  691.9 20.2 %copy-start.69 = (bf16[577,192]{0,1:T(8,128)(2,1)S(1)}, bf16[577,192]{0,1:T(8,128)(2,1)}, u32[]{:S(2)}) copy-start(bf16[577,192]{0,1:T(8,128)(2,1)} %copy-done.68) | copy-start | bytes 664708
  691.9 18.9 %all-to-all-start.5 = ((bf16[577,4,192]{0,2,1:T(8,128)(2,1)}), bf16[577,4,192]{0,2,1:T(8,128)(2,1)S(1)}, u32[]{:S(2)}, u32[]{:S(2)}) async-start(bf16[577,4,192]{0,2,1:T(8,128)(2,1)} %bitcast.38), calls=%async_computation.5 | async-start | bytes 1966080 | tf_op jit(solution)/shard_map/all_to_all | solution.py:53
  698.4 14.9 %copy-start.65 = (f32[577,192]{0,1:T(8,128)S(1)}, f32[577,192]{0,1:T(8,128)}, u32[]{:S(2)}) copy-start(f32[577,192]{0,1:T(8,128)} %get-tuple-element.63) | copy-start | bytes 1329412
  698.4 14.9 %copy-start.66 = (f32[577,192]{0,1:T(8,128)S(1)}, f32[577,192]{0,1:T(8,128)}, u32[]{:S(2)}) copy-start(f32[577,192]{0,1:T(8,128)} %get-tuple-element.61) | copy-start | bytes 1329412
  (92 other events, 185.4 us)
Sparse Core Ops, SparseCore 0:
  687.5 129.8 all-reduce.1
